TPU v7x, 256 devices: a whole 4x4x8 slice. The times are simulated.
256 devices in a mesh: row: 16 (over z, core), col: 16 (over y, x).
Axes of the slice: x: 4, y: 4, z: 8, core: 2. Of those that a mesh axis runs over, the one named last changes fastest.
Arguments:
- inputs: bfloat16 [2048, 8192], P('col', 'row'), may hold values from -6 to 6
- weight: bfloat16 [8192, 28672], P('row', 'col'), may hold values from -0.09375 to 0.09375
- mask: int32 [64, 224], P('row', 'col'), may hold values 0 or 1
- cotangent: bfloat16 [2048, 28672], P('row', 'col'), may hold values from -6 to 6
Outputs:
- outputs: bfloat16 [2048, 28672], P('row', 'col')
- input_grad: bfloat16 [2048, 8192], P('col', 'row')
- weight_grad: bfloat16 [8192, 28672], P('row', 'col')
Inputs may be any that keep to these rules, and one draw needn't show every extreme that they name: mask holds only zeros and ones.
All inputs are finite; a program needn't handle non-finite values. No bound on the sum of `mask` on one device may be relied on, other than what follows from the above.
Results may differ from a plain program's by a relative error of at most 0.022.
Values may be sent and summed in bfloat16 or wider, within the bound.
A program may use at most 128 MiB of HBM per device.

v0:
```python
import jax
import jax.numpy as jnp
from jax import lax
from jax.sharding import PartitionSpec as P

BLOCK = 128


def expand_mask(mask_tile):
    tile_rows, tile_cols = mask_tile.shape
    mask_bf16 = mask_tile.astype(jnp.bfloat16)
    widened = jnp.broadcast_to(mask_bf16[:, None, :, None], (tile_rows, BLOCK, tile_cols, BLOCK))
    return widened.reshape(tile_rows * BLOCK, tile_cols * BLOCK)


def local(inputs, weight, mask, cotangent):
    keep_mask = expand_mask(mask)
    masked = weight * keep_mask
    whole = lax.all_gather(inputs, "col", axis=0, tiled=True)
    token_total = whole.shape[0]
    chosen = whole
    outputs = lax.psum_scatter(
        jnp.dot(chosen, masked, preferred_element_type=jnp.float32).astype(jnp.bfloat16),
        "row",
        scatter_dimension=0,
        tiled=True,
    )
    shard_rows = lax.all_gather(cotangent, "row", axis=0, tiled=True)
    partial_value = lax.dot_general(
        shard_rows, masked, (((1,), (1,)), ((), ())), preferred_element_type=jnp.float32
    )
    grad_parts = partial_value.astype(jnp.bfloat16)
    chosen = whole
    weight_acc = lax.dot_general(
        chosen, shard_rows, (((0,), (0,)), ((), ())), preferred_element_type=jnp.float32
    )
    grad_parts, weight_acc = (grad_parts, weight_acc)
    summed = lax.psum_scatter(
        grad_parts.astype(jnp.float32).astype(jnp.bfloat16), "col", scatter_dimension=0, tiled=True
    )
    grad_scale = token_total ** (-0.5)
    weight_grad = (weight_acc * keep_mask.astype(jnp.float32) * grad_scale).astype(jnp.bfloat16)
    return (outputs, summed, weight_grad)


def solution(mesh):
    placed = (P("col", "row"), P("row", "col"), P("row", "col"), P("row", "col"))
    return jax.shard_map(
        local,
        mesh=mesh,
        in_specs=placed,
        out_specs=(P("row", "col"), P("col", "row"), P("row", "col")),
        check_vma=False,
    )
```

profile of v0, /device:TPU:10, one launch (start us, length us, event | category | flops | bytes accessed | tf_op | source)
XLA Modules:
  0.0 275.3 jit_solution(2744342380747078628)
XLA Ops:
  7.2 0.0 all-gather.5.cloned.1.call-start
  7.2 0.7 all-gather.5.cloned.1.call-update
  7.9 0.0 all-gather.3.cloned.1.call-start
  7.9 0.7 all-gather.3.cloned.1.call-update
  8.6 0.0 reduce-scatter.9.cloned.1.call-start
  8.7 0.7 convert_element_type.23
  9.4 0.1 copy.14
  9.5 3.8 %copy.15 = bf16[512,1792]{0,1:T(8,128)(2,1)} copy(bf16[512,1792]{1,0:T(8,128)(2,1)} %param.5) | data formatting | bytes 3670016 | tf_op args[1]
  13.3 50.4 %all-gather.5.cloned.1.call-done = bf16[2048,1792]{1,0:T(8,128)(2,1)} async-done(((bf16[128,1792]{1,0:T(8,128)(2,1)}), bf16[2048,1792]{1,0:T(8,128)(2,1)}) %all-gather.5.cloned.1.call-update) | async-done | bytes 7340048 | tf_op jit(solution)/shard_map/all_gather | solution.py:28
  63.7 0.5 broadcast_in_dim.2
  64.2 9.1 %fusion.1 = bf16[2048,512]{0,1:T(8,128)(2,1)} fusion(bf16[2048,1792]{1,0:T(8,128)(2,1)} %all-gather.5.cloned.1.call-done, bf16[512,1792]{0,1:T(8,128)(2,1)} %copy.15, bf16[224,8,4,128]{3,2,1,0:T(4,128)(2,1)S(1)} %bitcast.23), kind=kOutput, calls=%fused_computation.4 | convolution fusion | flops 3760062464 | bytes 13107200 | tf_op jit(solution)/shard_map/dot_general | solution.py:29
  73.3 4.0 %copy.21 = bf16[2048,512]{1,0:T(8,128)(2,1)} copy(bf16[2048,512]{0,1:T(8,128)(2,1)} %fusion.1) | data formatting | bytes 4194304
  77.3 0.0 reduce-scatter.9.cloned.1.call-update
  77.3 0.2 reduce-scatter.7.cloned.1.call-start
  77.5 35.6 %all-gather.3.cloned.1.call-done = bf16[2048,512]{1,0:T(8,128)(2,1)} async-done(((bf16[128,512]{1,0:T(8,128)(2,1)}), bf16[2048,512]{1,0:T(8,128)(2,1)}) %all-gather.3.cloned.1.call-update) | async-done | bytes 2097168 | tf_op jit(solution)/shard_map/all_gather | solution.py:19
  113.1 9.1 %fusion = bf16[2048,1792]{0,1:T(8,128)(2,1)} fusion(bf16[2048,512]{1,0:T(8,128)(2,1)} %all-gather.3.cloned.1.call-done, bf16[512,1792]{0,1:T(8,128)(2,1)} %copy.15, bf16[224,8,4,128]{3,2,1,0:T(4,128)(2,1)S(1)} %bitcast.24), kind=kOutput, calls=%fused_computation.1 | convolution fusion | flops 3762683904 | bytes 13107200 | tf_op jit(solution)/shard_map/dot_general | solution.py:23
  122.2 10.1 %copy.19 = bf16[2048,1792]{1,0:T(8,128)(2,1)} copy(bf16[2048,1792]{0,1:T(8,128)(2,1)} %fusion) | data formatting | bytes 14680064
  132.3 0.0 reduce-scatter.7.cloned.1.call-update
  132.3 1.5 copy.31
  133.9 2.8 %copy.16 = bf16[512,1792]{1,0:T(8,128)(2,1)S(1)} copy(bf16[512,1792]{0,1:T(8,128)(2,1)} %bitcast.26) | data formatting | bytes 3670016 | tf_op jit(solution)/shard_map/reshape | solution.py:13
  136.7 9.1 %multiply_convert_fusion = bf16[512,1792]{1,0:T(8,128)(2,1)} fusion(bf16[512,1792]{1,0:T(8,128)(2,1)S(1)} %copy.16, bf16[2048,512]{1,0:T(8,128)(2,1)} %all-gather.3.cloned.1.call-done, bf16[2048,1792]{1,0:T(8,128)(2,1)} %all-gather.5.cloned.1.call-done), kind=kOutput, calls=%fused_computation.2 | convolution fusion | flops 3761766400 | bytes 13107200 | tf_op jit(solution)/shard_map/dot_general | solution.py:34
  145.8 50.3 %reduce-scatter.9.cloned.1.call-done = bf16[128,512]{1,0:T(8,128)(2,1)} async-done(((bf16[2048,512]{1,0:T(8,128)(2,1)}), bf16[128,512]{1,0:T(8,128)(2,1)}) %reduce-scatter.9.cloned.1.call-update) | async-done | bytes 131088
  196.1 72.7 %reduce-scatter.7.cloned.1.call-done = bf16[128,1792]{1,0:T(8,128)(2,1)} async-done(((bf16[2048,1792]{1,0:T(8,128)(2,1)}), bf16[128,1792]{1,0:T(8,128)(2,1)}) %reduce-scatter.7.cloned.1.call-update) | async-done | bytes 458768
Async XLA Ops:
  7.2 56.5 %all-gather.5.cloned.1.call-start = ((), (), s32[]{:S(2)}) async-start(), calls=%async_computation.3 | async-start | bytes 7798784 | tf_op jit(solution)/shard_map/all_gather | solution.py:28
  7.9 105.2 %all-gather.3.cloned.1.call-start = ((), (), s32[]{:S(2)}) async-start(), calls=%async_computation.2 | async-start | bytes 2228224 | tf_op jit(solution)/shard_map/all_gather | solution.py:19
  8.6 187.4 %reduce-scatter.9.cloned.1.call-start = ((), (), s32[]{:S(2)}) async-start(), calls=%async_computation.5 | async-start | bytes 2228224
  77.3 191.5 %reduce-scatter.7.cloned.1.call-start = ((), (), s32[]{:S(2)}) async-start(), calls=%async_computation.4 | async-start | bytes 7798784
Sparse Core Ops, SparseCore 0:
  9.8 53.8 all-gather.4
  66.1 46.9 all-gather.2
  117.3 78.7 reduce-scatter.8
  199.2 69.5 reduce-scatter.6
where the time goes:
time: 276 us; the launch traced here: 275 us
  waiting for transfers between devices  210 us (76%)
  matrix products  27.2 us (10%)
  local copies, waits for them, and re-layouts  22.8 us (8%)
  between operations  13.8 us (5%)
    unnamed x6, waiting for transfers between devices  124 us
    all_gather x1, waiting for transfers between devices, local(): shard_rows = lax.all_gather(cotangent, 'row', axis=0, tiled=True)  50.4 us
    all_gather x1, waiting for transfers between devices, local(): whole = lax.all_gather(inputs, 'col', axis=0, tiled=True)  35.6 us
    unnamed x4, local copies, waits for them, and re-layouts  19.4 us
    dot_general x1, matrix products, local(): jnp.dot(chosen, masked, preferred_element_type=jnp.float32)  9.1 us
    dot_general x1, matrix products, local(): lax.dot_general(chosen, shard_rows, (((0,), (0,)), ((), ())), preferred_e...  9.08 us
    dot_general x1, matrix products, local(): lax.dot_general(shard_rows, masked, (((1,), (1,)), ((), ())), preferred_e...  9.06 us
  transfers between devices with their start and end apart: 4, of which 4 were waited for; matrix products, arithmetic and copies ran while one was open for 18% of the time, Pallas kernels for 0%

commit v1 on v0

--- a/solution.py
+++ b/solution.py
@@ -4,6 +4,32 @@
 from jax.sharding import PartitionSpec as P
 
 BLOCK = 128
+
+
+def mix_panels_here(body, join_dim):
+    item_now = lax.psum(1, "col")
+    after = lax.axis_index("col")
+    newest, current_arr, z_new = (item_now, after, body.shape[join_dim])
+    raw_out = jnp.zeros(
+        [p * newest if hop_no == join_dim else p for hop_no, p in enumerate(body.shape)], body.dtype
+    )
+    y1 = lax.dynamic_update_slice_in_dim(raw_out, body, current_arr * z_new, axis=join_dim)
+    plain = next_value = body
+    for no in range(1, newest // 2 + 1):
+        plain = lax.ppermute(
+            plain, "col", [(hop_no, (hop_no + 1) % newest) for hop_no in range(newest)]
+        )
+        y1 = lax.dynamic_update_slice_in_dim(
+            y1, plain, (current_arr - no) % newest * z_new, axis=join_dim
+        )
+        if 2 * no < newest:
+            next_value = lax.ppermute(
+                next_value, "col", [(hop_no, (hop_no - 1) % newest) for hop_no in range(newest)]
+            )
+            y1 = lax.dynamic_update_slice_in_dim(
+                y1, next_value, (current_arr + no) % newest * z_new, axis=join_dim
+            )
+    return y1
 
 
 def expand_mask(mask_tile):
@@ -16,7 +42,7 @@
 def local(inputs, weight, mask, cotangent):
     keep_mask = expand_mask(mask)
     masked = weight * keep_mask
-    whole = lax.all_gather(inputs, "col", axis=0, tiled=True)
+    whole = mix_panels_here(inputs, 0)
     token_total = whole.shape[0]
     chosen = whole
     outputs = lax.psum_scatter(

time: 276 us -> 241 us (0.87)
  waiting for transfers between devices: 210 us -> 160 us
  starting transfers between devices: 0.34 us -> 25.8 us
  local copies, waits for them, and re-layouts: 22.8 us -> 15.1 us
  matrix products: 27.2 us -> 23.7 us
    reduce_scatter x0 -> x1, waiting for transfers between devices: none -> 52.4 us  [local(): lax.psum_scatter(jnp.dot(chosen, masked, preferred_element_type=jnp.float...]
    all_gather x1, waiting for transfers between devices: 50.4 us -> 0.02 us  [local(): shard_rows = lax.all_gather(cotangent, 'row', axis=0, tiled=True)]
    unnamed x6 -> x4, waiting for transfers between devices: 124 us -> 81.3 us
    all_gather x1 -> x0, waiting for transfers between devices: 35.6 us -> none  [local(): whole = lax.all_gather(inputs, 'col', axis=0, tiled=True)]
    ppermute x0 -> x15, waiting for transfers between devices: none -> 26.2 us  [the longest x8 26.2 us: mix_panels_here(): lax.ppermute(plain, 'col', [(hop_no, (hop_no + 1) % newest) for hop_no in...]
    ppermute x0 -> x15, starting transfers between devices: none -> 25.6 us  [the longest x7 21.6 us: mix_panels_here(): lax.ppermute(next_value, 'col', [(hop_no, (hop_no - 1) % newest) for hop_...]
    unnamed x4 -> x11, local copies, waits for them, and re-layouts: 19.4 us -> 10.1 us
    dot_general x1, matrix products: 9.1 us -> 6.15 us  [local(): jnp.dot(chosen, masked, preferred_element_type=jnp.float32)]
  transfers between devices with their start and end apart: 4 -> 18, of which waited for: 4 -> 9; matrix products, arithmetic and copies ran while one was open for 18% -> 16% of each run, Pallas kernels for 0% -> 0%
where the time goes in v1:
time: 241 us; the launch traced here: 239 us
  waiting for transfers between devices  160 us (66%)
  starting transfers between devices  25.8 us (11%)
  matrix products  23.7 us (10%)
  local copies, waits for them, and re-layouts  15.1 us (6%)
  between operations  13.9 us (6%)
    unnamed x4, waiting for transfers between devices  81.3 us
    reduce_scatter x1, waiting for transfers between devices, local(): lax.psum_scatter(jnp.dot(chosen, masked, preferred_element_type=jnp.float...  52.4 us
    ppermute x8, waiting for transfers between devices, mix_panels_here(): lax.ppermute(plain, 'col', [(hop_no, (hop_no + 1) % newest) for hop_no in...  26.2 us
    ppermute x7, starting transfers between devices, mix_panels_here(): lax.ppermute(next_value, 'col', [(hop_no, (hop_no - 1) % newest) for hop_...  21.6 us
    unnamed x11, local copies, waits for them, and re-layouts  10.1 us
    dot_general x1, matrix products, local(): lax.dot_general(shard_rows, masked, (((1,), (1,)), ((), ())), preferred_e...  8.97 us
    dot_general x1, matrix products, local(): lax.dot_general(chosen, shard_rows, (((0,), (0,)), ((), ())), preferred_e...  8.55 us
    dot_general x1, matrix products, local(): jnp.dot(chosen, masked, preferred_element_type=jnp.float32)  6.15 us
  transfers between devices with their start and end apart: 18, of which 9 were waited for; matrix products, arithmetic and copies ran while one was open for 16% of the time, Pallas kernels for 0%

profile of v1, /device:TPU:10, one launch (start us, length us, event | category | flops | bytes accessed | tf_op | source)
XLA Modules:
  0.0 239.1 jit_solution(10909524214278542966)
XLA Ops:
  7.9 1.6 collective-permute-start
  10.8 3.9 %copy.13 = bf16[512,1792]{0,1:T(8,128)(2,1)} copy(bf16[512,1792]{1,0:T(8,128)(2,1)} %param.5) | data formatting | bytes 3670016 | tf_op args[1]
  14.9 1.6 collective-permute-start.2
  16.5 1.3 collective-permute-start.3
  17.8 2.8 %collective-permute-done.2 = bf16[128,512]{1,0:T(8,128)(2,1)S(1)} collective-permute-done((bf16[128,512]{1,0:T(8,128)(2,1)S(1)}, bf16[128,512]{1,0:T(8,128)(2,1)S(1)}, u32[]{:S(2)}, u32[]{:S(2)}) %collective-permute-start.2) | collective-permute-done | bytes 131104 | tf_op jit(solution)/shard_map/ppermute | solution.py:19
  21.4 3.3 %collective-permute-start.5 = (bf16[128,512]{1,0:T(8,128)(2,1)S(1)}, bf16[128,512]{1,0:T(8,128)(2,1)S(1)}, u32[]{:S(2)}, u32[]{:S(2)}) collective-permute-start(bf16[128,512]{1,0:T(8,128)(2,1)S(1)} %collective-permute-done.3), channel_id=1, source_target_pairs={{0,15},{1,0},{2,1},{3,2},{4,3},{5,4},{6,5},{7,6},{8,7},{9,8},{10,9... | collective-permute-start | bytes 393224 | tf_op jit(solution)/shard_map/ppermute | solution.py:26
  24.7 2.9 %collective-permute-done.4 = bf16[128,512]{1,0:T(8,128)(2,1)S(1)} collective-permute-done((bf16[128,512]{1,0:T(8,128)(2,1)S(1)}, bf16[128,512]{1,0:T(8,128)(2,1)S(1)}, u32[]{:S(2)}, u32[]{:S(2)}) %collective-permute-start.4) | collective-permute-done | bytes 131104 | tf_op jit(solution)/shard_map/ppermute | solution.py:19
  27.6 4.1 %collective-permute-start.7 = (bf16[128,512]{1,0:T(8,128)(2,1)S(1)}, bf16[128,512]{1,0:T(8,128)(2,1)S(1)}, u32[]{:S(2)}, u32[]{:S(2)}) collective-permute-start(bf16[128,512]{1,0:T(8,128)(2,1)S(1)} %collective-permute-done.5), channel_id=1, source_target_pairs={{0,15},{1,0},{2,1},{3,2},{4,3},{5,4},{6,5},{7,6},{8,7},{9,8},{10,9... | collective-permute-start | bytes 393224 | tf_op jit(solution)/shard_map/ppermute | solution.py:26
  31.8 2.9 %collective-permute-done.6 = bf16[128,512]{1,0:T(8,128)(2,1)S(1)} collective-permute-done((bf16[128,512]{1,0:T(8,128)(2,1)S(1)}, bf16[128,512]{1,0:T(8,128)(2,1)S(1)}, u32[]{:S(2)}, u32[]{:S(2)}) %collective-permute-start.6) | collective-permute-done | bytes 131104 | tf_op jit(solution)/shard_map/ppermute | solution.py:19
  34.7 4.1 %collective-permute-start.9 = (bf16[128,512]{1,0:T(8,128)(2,1)S(1)}, bf16[128,512]{1,0:T(8,128)(2,1)S(1)}, u32[]{:S(2)}, u32[]{:S(2)}) collective-permute-start(bf16[128,512]{1,0:T(8,128)(2,1)S(1)} %collective-permute-done.7), channel_id=1, source_target_pairs={{0,15},{1,0},{2,1},{3,2},{4,3},{5,4},{6,5},{7,6},{8,7},{9,8},{10,9... | collective-permute-start | bytes 393224 | tf_op jit(solution)/shard_map/ppermute | solution.py:26
  38.9 3.2 %collective-permute-done.8 = bf16[128,512]{1,0:T(8,128)(2,1)S(1)} collective-permute-done((bf16[128,512]{1,0:T(8,128)(2,1)S(1)}, bf16[128,512]{1,0:T(8,128)(2,1)S(1)}, u32[]{:S(2)}, u32[]{:S(2)}) %collective-permute-start.8) | collective-permute-done | bytes 131104 | tf_op jit(solution)/shard_map/ppermute | solution.py:19
  42.1 4.5 %collective-permute-start.11 = (bf16[128,512]{1,0:T(8,128)(2,1)S(1)}, bf16[128,512]{1,0:T(8,128)(2,1)S(1)}, u32[]{:S(2)}, u32[]{:S(2)}) collective-permute-start(bf16[128,512]{1,0:T(8,128)(2,1)S(1)} %collective-permute-done.9), channel_id=1, source_target_pairs={{0,15},{1,0},{2,1},{3,2},{4,3},{5,4},{6,5},{7,6},{8,7},{9,8},{10,9... | collective-permute-start | bytes 393224 | tf_op jit(solution)/shard_map/ppermute | solution.py:26
  46.6 4.3 %collective-permute-done.10 = bf16[128,512]{1,0:T(8,128)(2,1)S(1)} collective-permute-done((bf16[128,512]{1,0:T(8,128)(2,1)S(1)}, bf16[128,512]{1,0:T(8,128)(2,1)S(1)}, u32[]{:S(2)}, u32[]{:S(2)}) %collective-permute-start.10) | collective-permute-done | bytes 131104 | tf_op jit(solution)/shard_map/ppermute | solution.py:19
  50.9 3.9 %collective-permute-start.13 = (bf16[128,512]{1,0:T(8,128)(2,1)S(1)}, bf16[128,512]{1,0:T(8,128)(2,1)S(1)}, u32[]{:S(2)}, u32[]{:S(2)}) collective-permute-start(bf16[128,512]{1,0:T(8,128)(2,1)S(1)} %collective-permute-done.11), channel_id=1, source_target_pairs={{0,15},{1,0},{2,1},{3,2},{4,3},{5,4},{6,5},{7,6},{8,7},{9,8},{10,9... | collective-permute-start | bytes 393224 | tf_op jit(solution)/shard_map/ppermute | solution.py:26
  54.8 3.4 %collective-permute-done.12 = bf16[128,512]{1,0:T(8,128)(2,1)S(1)} collective-permute-done((bf16[128,512]{1,0:T(8,128)(2,1)S(1)}, bf16[128,512]{1,0:T(8,128)(2,1)S(1)}, u32[]{:S(2)}, u32[]{:S(2)}) %collective-permute-start.12) | collective-permute-done | bytes 131104 | tf_op jit(solution)/shard_map/ppermute | solution.py:19
  58.2 6.7 %collective-permute-done.14 = bf16[128,512]{1,0:T(8,128)(2,1)S(1)} collective-permute-done((bf16[128,512]{1,0:T(8,128)(2,1)S(1)}, bf16[128,512]{1,0:T(8,128)(2,1)S(1)}, u32[]{:S(2)}, u32[]{:S(2)}) %collective-permute-start.14) | collective-permute-done | bytes 131104 | tf_op jit(solution)/shard_map/ppermute | solution.py:19
  66.3 6.2 %convolution_convert_fusion = bf16[2048,1792]{1,0:T(8,128)(2,1)} fusion(bf16[2048,512]{1,0:T(8,128)(2,1)S(1)} %constant_dynamic-update-slice_fusion, bf16[512,1792]{0,1:T(8,128)(2,1)S(1)} %copy-done.2, bf16[224,8,4,128]{3,2,1,0:T(4,128)(2,1)S(1)} %bitcast.20), kind=kOutput, calls=%fused_computation | convolution fusion | flops 3762683904 | bytes 13107200 | tf_op jit(solution)/shard_map/dot_general | solution.py:49
  72.6 9.0 %fusion = bf16[2048,512]{0,1:T(8,128)(2,1)} fusion(bf16[2048,1792]{1,0:T(8,128)(2,1)} %all-gather.2.cloned.1.call-done, bf16[512,1792]{0,1:T(8,128)(2,1)} %copy.13, bf16[224,8,4,128]{3,2,1,0:T(4,128)(2,1)S(1)} %bitcast.21), kind=kOutput, calls=%fused_computation.3 | convolution fusion | flops 3760062464 | bytes 13107200 | tf_op jit(solution)/shard_map/dot_general | solution.py:55
  81.6 3.9 %copy.16 = bf16[2048,512]{1,0:T(8,128)(2,1)} copy(bf16[2048,512]{0,1:T(8,128)(2,1)} %fusion) | data formatting | bytes 4194304
  85.5 1.5 copy.26
  87.0 4.0 %copy.14 = bf16[512,1792]{1,0:T(8,128)(2,1)} copy(bf16[512,1792]{0,1:T(8,128)(2,1)} %bitcast.23) | data formatting | bytes 3670016 | tf_op jit(solution)/shard_map/reshape | solution.py:39
  91.1 8.6 %multiply_convert_fusion = bf16[512,1792]{1,0:T(8,128)(2,1)} fusion(bf16[512,1792]{1,0:T(8,128)(2,1)} %copy.14, bf16[2048,512]{1,0:T(8,128)(2,1)S(1)} %copy-done.1, bf16[2048,1792]{1,0:T(8,128)(2,1)} %all-gather.2.cloned.1.call-done), kind=kOutput, calls=%fused_computation.1 | convolution fusion | flops 3761766400 | bytes 13107200 | tf_op jit(solution)/shard_map/dot_general | solution.py:60
  99.6 52.4 %reduce-scatter.5.cloned.1.call-done = bf16[128,1792]{1,0:T(8,128)(2,1)} async-done(((bf16[2048,1792]{1,0:T(8,128)(2,1)}), bf16[128,1792]{1,0:T(8,128)(2,1)}) %reduce-scatter.5.cloned.1.call-update) | async-done | bytes 458768 | tf_op jit(solution)/shard_map/reduce_scatter | solution.py:48
  152.0 80.6 %reduce-scatter.7.cloned.1.call-done = bf16[128,512]{1,0:T(8,128)(2,1)} async-done(((bf16[2048,512]{1,0:T(8,128)(2,1)}), bf16[128,512]{1,0:T(8,128)(2,1)}) %reduce-scatter.7.cloned.1.call-update) | async-done | bytes 131088
  (50 shorter events, 4.8 us)
Async XLA Ops:
  7.2 65.4 %all-gather.2.cloned.1.call-start = ((), (), s32[]{:S(2)}) async-start(), calls=%async_computation.3 | async-start | bytes 7798784 | tf_op jit(solution)/shard_map/all_gather | solution.py:54
  7.9 144.1 %reduce-scatter.5.cloned.1.call-start = ((), (), s32[]{:S(2)}) async-start(), calls=%async_computation.2 | async-start | bytes 7798784 | tf_op jit(solution)/shard_map/reduce_scatter | solution.py:48
  7.9 6.9 %collective-permute-start = (bf16[128,512]{1,0:T(8,128)(2,1)}, bf16[128,512]{1,0:T(8,128)(2,1)S(1)}, u32[]{:S(2)}, u32[]{:S(2)}) collective-permute-start(bf16[128,512]{1,0:T(8,128)(2,1)} %param.4), channel_id=1, source_target_pairs={{0,1},{1,2},{2,3},{3,4},{4,5},{5,6},{6,7},{7,8},{8,9},{9,10},{10,1... | collective-permute-start | bytes 393224 | tf_op jit(solution)/shard_map/ppermute | solution.py:19
  9.5 7.0 %collective-permute-start.1 = (bf16[128,512]{1,0:T(8,128)(2,1)}, bf16[128,512]{1,0:T(8,128)(2,1)S(1)}, u32[]{:S(2)}, u32[]{:S(2)}) collective-permute-start(bf16[128,512]{1,0:T(8,128)(2,1)} %param.4), channel_id=1, source_target_pairs={{0,15},{1,0},{2,1},{3,2},{4,3},{5,4},{6,5},{7,6},{8,7},{9,8},{10,9... | collective-permute-start | bytes 393224 | tf_op jit(solution)/shard_map/ppermute | solution.py:26
  10.8 4.0 %copy-start.3 = (bf16[128,512]{1,0:T(8,128)(2,1)S(1)}, bf16[128,512]{1,0:T(8,128)(2,1)}, u32[]{:S(2)}) copy-start(bf16[128,512]{1,0:T(8,128)(2,1)} %param.4) | copy-start | bytes 393220
  14.9 5.7 %collective-permute-start.2 = (bf16[128,512]{1,0:T(8,128)(2,1)S(1)}, bf16[128,512]{1,0:T(8,128)(2,1)S(1)}, u32[]{:S(2)}, u32[]{:S(2)}) collective-permute-start(bf16[128,512]{1,0:T(8,128)(2,1)S(1)} %collective-permute-done), channel_id=1, source_target_pairs={{0,1},{1,2},{2,3},{3,4},{4,5},{5,6},{6,7},{7,8},{8,9},{9,10},{10,1... | collective-permute-start | bytes 393224 | tf_op jit(solution)/shard_map/ppermute | solution.py:19
  16.5 5.0 %collective-permute-start.3 = (bf16[128,512]{1,0:T(8,128)(2,1)S(1)}, bf16[128,512]{1,0:T(8,128)(2,1)S(1)}, u32[]{:S(2)}, u32[]{:S(2)}) collective-permute-start(bf16[128,512]{1,0:T(8,128)(2,1)S(1)} %collective-permute-done.1), channel_id=1, source_target_pairs={{0,15},{1,0},{2,1},{3,2},{4,3},{5,4},{6,5},{7,6},{8,7},{9,8},{10,9... | collective-permute-start | bytes 393224 | tf_op jit(solution)/shard_map/ppermute | solution.py:26
  20.6 7.1 %collective-permute-start.4 = (bf16[128,512]{1,0:T(8,128)(2,1)S(1)}, bf16[128,512]{1,0:T(8,128)(2,1)S(1)}, u32[]{:S(2)}, u32[]{:S(2)}) collective-permute-start(bf16[128,512]{1,0:T(8,128)(2,1)S(1)} %collective-permute-done.2), channel_id=1, source_target_pairs={{0,1},{1,2},{2,3},{3,4},{4,5},{5,6},{6,7},{7,8},{8,9},{9,10},{10,1... | collective-permute-start | bytes 393224 | tf_op jit(solution)/shard_map/ppermute | solution.py:19
  21.4 6.2 %collective-permute-start.5 = (bf16[128,512]{1,0:T(8,128)(2,1)S(1)}, bf16[128,512]{1,0:T(8,128)(2,1)S(1)}, u32[]{:S(2)}, u32[]{:S(2)}) collective-permute-start(bf16[128,512]{1,0:T(8,128)(2,1)S(1)} %collective-permute-done.3), channel_id=1, source_target_pairs={{0,15},{1,0},{2,1},{3,2},{4,3},{5,4},{6,5},{7,6},{8,7},{9,8},{10,9... | collective-permute-start | bytes 393224 | tf_op jit(solution)/shard_map/ppermute | solution.py:26
  27.6 7.1 %collective-permute-start.6 = (bf16[128,512]{1,0:T(8,128)(2,1)S(1)}, bf16[128,512]{1,0:T(8,128)(2,1)S(1)}, u32[]{:S(2)}, u32[]{:S(2)}) collective-permute-start(bf16[128,512]{1,0:T(8,128)(2,1)S(1)} %collective-permute-done.4), channel_id=1, source_target_pairs={{0,1},{1,2},{2,3},{3,4},{4,5},{5,6},{6,7},{7,8},{8,9},{9,10},{10,1... | collective-permute-start | bytes 393224 | tf_op jit(solution)/shard_map/ppermute | solution.py:19
  27.6 7.1 %collective-permute-start.7 = (bf16[128,512]{1,0:T(8,128)(2,1)S(1)}, bf16[128,512]{1,0:T(8,128)(2,1)S(1)}, u32[]{:S(2)}, u32[]{:S(2)}) collective-permute-start(bf16[128,512]{1,0:T(8,128)(2,1)S(1)} %collective-permute-done.5), channel_id=1, source_target_pairs={{0,15},{1,0},{2,1},{3,2},{4,3},{5,4},{6,5},{7,6},{8,7},{9,8},{10,9... | collective-permute-start | bytes 393224 | tf_op jit(solution)/shard_map/ppermute | solution.py:26
  31.8 34.5 %copy-start.2 = (bf16[512,1792]{0,1:T(8,128)(2,1)S(1)}, bf16[512,1792]{0,1:T(8,128)(2,1)}, u32[]{:S(2)}) copy-start(bf16[512,1792]{0,1:T(8,128)(2,1)} %copy.13) | copy-start | bytes 5505028
  34.7 7.3 %collective-permute-start.8 = (bf16[128,512]{1,0:T(8,128)(2,1)S(1)}, bf16[128,512]{1,0:T(8,128)(2,1)S(1)}, u32[]{:S(2)}, u32[]{:S(2)}) collective-permute-start(bf16[128,512]{1,0:T(8,128)(2,1)S(1)} %collective-permute-done.6), channel_id=1, source_target_pairs={{0,1},{1,2},{2,3},{3,4},{4,5},{5,6},{6,7},{7,8},{8,9},{9,10},{10,1... | collective-permute-start | bytes 393224 | tf_op jit(solution)/shard_map/ppermute | solution.py:19
  34.7 7.3 %collective-permute-start.9 = (bf16[128,512]{1,0:T(8,128)(2,1)S(1)}, bf16[128,512]{1,0:T(8,128)(2,1)S(1)}, u32[]{:S(2)}, u32[]{:S(2)}) collective-permute-start(bf16[128,512]{1,0:T(8,128)(2,1)S(1)} %collective-permute-done.7), channel_id=1, source_target_pairs={{0,15},{1,0},{2,1},{3,2},{4,3},{5,4},{6,5},{7,6},{8,7},{9,8},{10,9... | collective-permute-start | bytes 393224 | tf_op jit(solution)/shard_map/ppermute | solution.py:26
  42.1 8.8 %collective-permute-start.10 = (bf16[128,512]{1,0:T(8,128)(2,1)S(1)}, bf16[128,512]{1,0:T(8,128)(2,1)S(1)}, u32[]{:S(2)}, u32[]{:S(2)}) collective-permute-start(bf16[128,512]{1,0:T(8,128)(2,1)S(1)} %collective-permute-done.8), channel_id=1, source_target_pairs={{0,1},{1,2},{2,3},{3,4},{4,5},{5,6},{6,7},{7,8},{8,9},{9,10},{10,1... | collective-permute-start | bytes 393224 | tf_op jit(solution)/shard_map/ppermute | solution.py:19
  42.1 8.8 %collective-permute-start.11 = (bf16[128,512]{1,0:T(8,128)(2,1)S(1)}, bf16[128,512]{1,0:T(8,128)(2,1)S(1)}, u32[]{:S(2)}, u32[]{:S(2)}) collective-permute-start(bf16[128,512]{1,0:T(8,128)(2,1)S(1)} %collective-permute-done.9), channel_id=1, source_target_pairs={{0,15},{1,0},{2,1},{3,2},{4,3},{5,4},{6,5},{7,6},{8,7},{9,8},{10,9... | collective-permute-start | bytes 393224 | tf_op jit(solution)/shard_map/ppermute | solution.py:26
  50.9 7.3 %collective-permute-start.12 = (bf16[128,512]{1,0:T(8,128)(2,1)S(1)}, bf16[128,512]{1,0:T(8,128)(2,1)S(1)}, u32[]{:S(2)}, u32[]{:S(2)}) collective-permute-start(bf16[128,512]{1,0:T(8,128)(2,1)S(1)} %collective-permute-done.10), channel_id=1, source_target_pairs={{0,1},{1,2},{2,3},{3,4},{4,5},{5,6},{6,7},{7,8},{8,9},{9,10},{10,1... | collective-permute-start | bytes 393224 | tf_op jit(solution)/shard_map/ppermute | solution.py:19
  50.9 7.3 %collective-permute-start.13 = (bf16[128,512]{1,0:T(8,128)(2,1)S(1)}, bf16[128,512]{1,0:T(8,128)(2,1)S(1)}, u32[]{:S(2)}, u32[]{:S(2)}) collective-permute-start(bf16[128,512]{1,0:T(8,128)(2,1)S(1)} %collective-permute-done.11), channel_id=1, source_target_pairs={{0,15},{1,0},{2,1},{3,2},{4,3},{5,4},{6,5},{7,6},{8,7},{9,8},{10,9... | collective-permute-start | bytes 393224 | tf_op jit(solution)/shard_map/ppermute | solution.py:26
  58.2 6.8 %collective-permute-start.14 = (bf16[128,512]{1,0:T(8,128)(2,1)S(1)}, bf16[128,512]{1,0:T(8,128)(2,1)S(1)}, u32[]{:S(2)}, u32[]{:S(2)}) collective-permute-start(bf16[128,512]{1,0:T(8,128)(2,1)S(1)} %collective-permute-done.12), channel_id=1, source_target_pairs={{0,1},{1,2},{2,3},{3,4},{4,5},{5,6},{6,7},{7,8},{8,9},{9,10},{10,1... | collective-permute-start | bytes 393224 | tf_op jit(solution)/shard_map/ppermute | solution.py:19
  65.0 1.3 copy-start
  72.5 160.1 %reduce-scatter.7.cloned.1.call-start = ((), (), s32[]{:S(2)}) async-start(), calls=%async_computation.4 | async-start | bytes 2228224
  87.0 4.0 %copy-start.1 = (bf16[2048,512]{1,0:T(8,128)(2,1)S(1)}, bf16[2048,512]{1,0:T(8,128)(2,1)}, u32[]{:S(2)}) copy-start(bf16[2048,512]{1,0:T(8,128)(2,1)} %copy-done) | copy-start | bytes 6291460
Sparse Core Ops, SparseCore 0:
  9.8 53.8 all-gather.1
  72.6 79.3 reduce-scatter.4
  156.1 76.4 reduce-scatter.6
